TPU v7x, 32 devices: a whole 2x2x4 slice. The times are simulated.
32 devices in a mesh: group: 8 (over z, core), dp: 4 (over y, x).
Axes of the slice: x: 2, y: 2, z: 4, core: 2. Of those that a mesh axis runs over, the one named last changes fastest.
Arguments:
- resp_q: bfloat16 [8, 1024, 4096], P('group', 'dp'), may hold values from -410 to 410
- resp_k: bfloat16 [8, 1024, 4096], P('group', 'dp'), may hold values from -410 to 410
- resp_v: bfloat16 [8, 1024, 4096], P('group', 'dp'), may hold values from -6 to 6
- prompt_k: bfloat16 [8, 512, 4096], P('group', 'dp'), may hold values from -410 to 410
- prompt_v: bfloat16 [8, 512, 4096], P('group', 'dp'), may hold values from -6 to 6
- prompt_len: int32 [8], P('group'), may hold values from 128 to 512
- resp_len: int32 [8, 4], P('group', 'dp'), may hold values from 1 to 256, as said below
- assign: int32 [8, 8], P('group', 'dp'), may hold values from 0 to 15, as said below
- rewards: float32 [8, 4], P('group', 'dp'), may hold values from -18 to 18
- feat_q: bfloat16 [32, 128, 128], replicated, may hold values from -1 to 1
- feat_k: bfloat16 [32, 128, 128], replicated, may hold values from -1 to 1
Outputs:
- attn_out: bfloat16 [8, 512, 4096], P('group', 'dp')
- token_adv: float32 [8, 512], P('group', 'dp')
Inputs may be any that keep to these rules, and one draw needn't show every extreme that they name: Response r of a prompt has ceil(resp_len / 64) live blocks; these counts sum to 2 * 4 over a prompt's responses, and one response of every prompt has 4 blocks. `assign`: entry d * 2 + j names the block r * 4 + c (block c of response r) whose outputs go to slot j of device d of dp. Every live block of the prompt is named exactly once, and the 2 slots of one device name blocks of different responses.
All inputs are finite; a program needn't handle non-finite values.
Results may differ from a plain program's by a relative error of at most 0.0085.
Values may be sent and summed in bfloat16 or wider, within the bound.
A program may use at most 128 MiB of HBM per device.

v0:
```python
import jax
import jax.numpy as jnp
from jax import lax
from jax.sharding import PartitionSpec as P

BLK = 64


def features(rows, weights):
    logits = jnp.einsum("thd,hdf->thf", rows, weights, preferred_element_type=jnp.float32)
    return jnp.concatenate(
        [jax.nn.softmax(logits, axis=-1), jax.nn.softmax(-logits, axis=-1)], axis=-1
    ).astype(jnp.bfloat16)


def state_terms(query_feat, state_rounded, total_rounded):
    numerator = jnp.einsum(
        "thf,hfe->the", query_feat, state_rounded, preferred_element_type=jnp.float32
    )
    denominator = jnp.einsum(
        "thf,hf->th", query_feat, total_rounded, preferred_element_type=jnp.float32
    )
    return (numerator.astype(jnp.bfloat16), denominator.astype(jnp.bfloat16))


def body(
    resp_q,
    resp_k,
    resp_v,
    prompt_k,
    prompt_v,
    prompt_len,
    resp_len,
    assign,
    rewards,
    feat_q,
    feat_k,
):
    dp_count = lax.axis_size("dp")
    my_index = lax.axis_index("dp")
    head_count = feat_q.shape[0]
    head_width = feat_q.shape[1]
    length = resp_q.shape[1]
    prompt_rows = prompt_k.shape[1]
    queries = resp_q[0].reshape(length, head_count, head_width)
    key_rows = resp_k[0].reshape(length, head_count, head_width)
    values = resp_v[0].reshape(length, head_count, head_width)
    prompt_keys = prompt_k[0].reshape(prompt_rows, head_count, head_width)
    prompt_values = prompt_v[0].reshape(prompt_rows, head_count, head_width)
    keep = my_index * prompt_rows + jnp.arange(prompt_rows) < prompt_len[0]
    prompt_feat = jnp.where(
        keep[:, None, None], features(prompt_keys, feat_k), jnp.zeros((), jnp.bfloat16)
    )
    part_state = jnp.einsum(
        "shf,she->hfe", prompt_feat, prompt_values, preferred_element_type=jnp.float32
    )
    part_total = jnp.sum(prompt_feat.astype(jnp.float32), axis=0)
    query_feat = features(queries, feat_q)
    key_feat = features(key_rows, feat_k)
    kv_share, total_share = (
        lax.psum_scatter(part_state, "dp", scatter_dimension=0, tiled=True),
        lax.psum_scatter(part_total, "dp", scatter_dimension=0, tiled=True),
    )
    kv_state, key_total = (
        lax.all_gather(kv_share.astype(jnp.bfloat16), "dp", axis=0, tiled=True),
        lax.all_gather(total_share.astype(jnp.bfloat16), "dp", axis=0, tiled=True),
    )
    prompt_num, prompt_den = state_terms(query_feat, kv_state, key_total)
    causal = jnp.arange(length)[:, None] >= jnp.arange(length)[None, :]
    scores = jnp.einsum("thf,shf->hts", query_feat, key_feat, preferred_element_type=jnp.float32)
    scores = jnp.where(causal[None], scores, jnp.float32(0.0))
    intra_den = jnp.sum(scores, axis=-1)
    intra_num = jnp.einsum(
        "hts,she->the", scores.astype(jnp.bfloat16), values, preferred_element_type=jnp.float32
    )
    combined = (prompt_num.astype(jnp.float32) + intra_num) / (
        prompt_den.astype(jnp.float32) + intra_den.T
    )[:, :, None]
    live_rows = jnp.arange(length) < resp_len[0, 0]
    combined = jnp.where(live_rows[:, None, None], combined, jnp.float32(0.0))
    result = combined.astype(jnp.bfloat16).reshape(-1, BLK, head_count * head_width)
    pieces = result.shape[0]
    slot_width = assign.shape[1]
    table, lengths = (
        lax.all_gather(assign, "dp", axis=1, tiled=True),
        lax.all_gather(resp_len, "dp", axis=1, tiled=True),
    )
    slot_ids = table[0].reshape(dp_count, slot_width)
    own_ids = assign[0]
    source = own_ids // pieces
    stretch_index = own_ids % pieces
    picker = source[:, None] == jnp.arange(dp_count)[None, :]
    mine_mask = jnp.any(
        slot_ids[:, :, None] == my_index * pieces + jnp.arange(pieces)[None, None, :], axis=1
    )
    outgoing = jnp.einsum(
        "dc,cbe->dbe", mine_mask.astype(jnp.bfloat16), result, preferred_element_type=jnp.float32
    ).astype(jnp.bfloat16)
    incoming = lax.all_to_all(outgoing, "dp", split_axis=0, concat_axis=0, tiled=True)
    attended = jnp.einsum(
        "jd,dbe->jbe", picker.astype(jnp.bfloat16), incoming, preferred_element_type=jnp.float32
    ).astype(jnp.bfloat16)
    attended = attended.reshape(1, slot_width * BLK, head_count * head_width)
    reward_all = lax.all_gather(rewards, "dp", axis=1, tiled=True)[0]
    centred = reward_all - jnp.sum(reward_all) / dp_count
    spread = lax.psum(jnp.sum(centred * centred), "group")
    advantage = centred / jnp.sqrt(spread / (lax.axis_size("group") * dp_count) + 1e-06)
    slot_adv = jnp.sum(jnp.where(picker, advantage[None, :], jnp.float32(0.0)), axis=1)
    slot_len = jnp.sum(jnp.where(picker, lengths[0][None, :], 0), axis=1)
    positions = stretch_index[:, None] * BLK + jnp.arange(BLK)[None, :]
    token_adv = jnp.where(positions < slot_len[:, None], slot_adv[:, None], jnp.float32(0.0))
    return (attended, token_adv.reshape(1, slot_width * BLK))


def solution(mesh):
    return jax.shard_map(
        body,
        mesh=mesh,
        in_specs=(
            P("group", "dp", None),
            P("group", "dp", None),
            P("group", "dp", None),
            P("group", "dp", None),
            P("group", "dp", None),
            P("group"),
            P("group", "dp"),
            P("group", "dp"),
            P("group", "dp"),
            P(),
            P(),
        ),
        out_specs=(P("group", "dp", None), P("group", "dp")),
        check_vma=False,
    )
```

profile of v0, /device:TPU:0, one launch (start us, length us, event | category | flops | bytes accessed | tf_op | source)
XLA Modules:
  0.0 187.2 jit_solution(10308482313674577774)
XLA Ops:
  8.8 2.5 %fusion.63 = (f32[128,32]{0,1:T(8,128)S(1)}, f32[128,32,128]{0,2,1:T(8,128)}) fusion(bf16[32,128,128]{2,1,0:T(8,128)(2,1)S(1)} %copy-done, bf16[128,32,128]{2,1,0:T(8,128)(2,1)S(1)} %bitcast.135), kind=kOutput, calls=%fused_computation.102 | convolution fusion | flops 135790720 | bytes 4210688 | tf_op jit(solution)/shard_map/sub | solution.py:12
  14.7 2.4 %copy.92 = bf16[16,8,32,128]{3,2,1,0:T(8,128)(2,1)} copy(bf16[16,8,32,128]{3,1,2,0:T(8,128)(2,1)} %bitcast.142) | data formatting | bytes 2097152
  20.8 2.8 %fusion.38 = f32[32,256,128]{2,1,0:T(8,128)} fusion(bf16[128,32,128]{0,2,1:T(8,128)(2,1)S(1)} %get-tuple-element.29, bf16[128,32,128]{0,2,1:T(8,128)(2,1)S(1)} %get-tuple-element.30, pred[128]{0:T(512)(128)(4,1)S(1)} %add_compare_fusion, bf16[128,32,128]{2,1,0:T(8,128)(2,1)S(1)} %bitcast.143), kind=kOutput, calls=%fused_computation.58 | convolution fusion | flops 273678336 | bytes 7340160 | tf_op jit(solution)/shard_map/shf,she->hfe/dot_general | solution.py:54
  26.1 8.9 %all-reduce.4 = (s32[8]{0:T(128)S(1)}, s32[4]{0:T(128)S(1)}) all-reduce(s32[8]{0:T(128)S(1)} %get-tuple-element.8, s32[4]{0:T(128)S(1)} %bitcast_dynamic-update-slice_fusion.1), channel_id=1, replica_groups=mesh['group'=8,'dp'=4] {'dp'}, use_global_device_ids=true, to_apply=%add | all-reduce | flops 12 | bytes 96
  37.2 3.4 %copy.93 = bf16[32,8,32,128]{3,2,1,0:T(8,128)(2,1)} copy(bf16[32,8,32,128]{3,1,2,0:T(8,128)(2,1)} %bitcast.138) | data formatting | bytes 4194304
  44.5 2.4 %convert_reduce_fusion = f32[32,256]{1,0:T(8,128)S(1)} fusion(bf16[128,32,128]{0,2,1:T(8,128)(2,1)} %copy-done.4, bf16[128,32,128]{0,2,1:T(8,128)(2,1)} %copy-done.5, pred[128]{0:T(512)(128)(4,1)S(1)} %add_compare_fusion), kind=kLoop, calls=%fused_computation.30 | loop fusion | flops 7331840 | bytes 2130048 | tf_op jit(solution)/shard_map/reduce_sum | solution.py:57
  46.9 16.8 %all-reduce.5 = (bf16[32,256]{1,0:T(8,128)(2,1)S(1)}, f32[4]{0:T(128)S(1)}) all-reduce(f32[32,256]{1,0:T(8,128)S(1)} %convert_reduce_fusion, f32[4]{0:T(128)S(1)} %bitcast_dynamic-update-slice_fusion), channel_id=3, replica_groups=mesh['group'=8,'dp'=4] {'dp'}, use_global_device_ids=true, to_apply=%region_15.16.clone | all-reduce | flops 8196 | bytes 49184
  63.7 8.6 %all_gather.17 = bf16[32,256]{1,0:T(8,128)(2,1)S(1)} all-gather(bf16[8,256]{1,0:T(8,128)(2,1)S(1)} %dynamic-slice_convert_fusion), channel_id=1, replica_groups=mesh['group'=8,'dp'=4] {'dp'}, dimensions={0}, use_global_device_ids=true | all-gather | bytes 20480 | tf_op jit(solution)/shard_map/all_gather | solution.py:66
  72.5 3.2 %fusion.31 = f32[32,128,256]{2,1,0:T(8,128)S(1)} fusion(bf16[32,128,128]{2,1,0:T(8,128)(2,1)} %param.20, bf16[256,32,128]{2,1,0:T(8,128)(2,1)} %bitcast.134), kind=kOutput, calls=%fused_computation.50 | convolution fusion | flops 268435456 | bytes 7340032 | tf_op jit(solution)/shard_map/thd,hdf->thf/dot_general | solution.py:10
  75.7 4.0 %fusion.61 = (f32[256,32]{0,1:T(8,128)S(1)}, f32[256,32,128]{0,2,1:T(8,128)S(1)}) fusion(f32[32,128,256]{2,1,0:T(8,128)S(1)} %fusion.31), kind=kOutput, calls=%fused_computation.100 | output fusion | flops 4194431 | bytes 8421376 | tf_op jit(solution)/shard_map/sub | solution.py:12
  79.7 3.9 %fusion.62 = (f32[256,32]{0,1:T(8,128)S(1)}, f32[256,32,128]{0,2,1:T(8,128)S(1)}) fusion(f32[32,128,256]{2,1,0:T(8,128)S(1)} %fusion.31), kind=kOutput, calls=%fused_computation.101 | output fusion | flops 2097279 | bytes 8421376 | tf_op jit(solution)/shard_map/sub | solution.py:12
  88.9 3.0 %fusion.59 = (f32[256,32]{0,1:T(8,128)S(1)}, f32[256,32,128]{0,2,1:T(8,128)}) fusion(f32[32,128,256]{2,1,0:T(8,128)S(1)} %fusion.29), kind=kOutput, calls=%fused_computation.98 | output fusion | flops 4194431 | bytes 8421376 | tf_op jit(solution)/shard_map/sub | solution.py:12
  94.1 4.4 %fusion.60 = (f32[256,32]{0,1:T(8,128)S(1)}, f32[256,32,128]{0,2,1:T(8,128)S(1)}) fusion(f32[32,128,256]{2,1,0:T(8,128)} %copy-done.2), kind=kOutput, calls=%fused_computation.99 | output fusion | flops 2097279 | bytes 8421376 | tf_op jit(solution)/shard_map/sub | solution.py:12
  98.8 3.2 %divide_convert_fusion = (bf16[256,32,128]{0,2,1:T(8,128)(2,1)}, bf16[256,32,128]{0,2,1:T(8,128)(2,1)}) fusion(f32[256,32,128]{0,2,1:T(8,128)S(1)} %copy-done.3, f32[256,32]{0,1:T(8,128)S(1)} %get-tuple-element.11, f32[256,32,128]{0,2,1:T(8,128)S(1)} %get-tuple-element.14, f32[256,32]{0,1:T(8,128)S(1)} %get-tuple-element.13), kind=kLoop, calls=%fused_computation.32 | loop fusion | flops 4194304 | bytes 12648448 | tf_op jit(solution)/shard_map/convert.2
  102.0 5.3 %select_reduce_fusion = (f32[32,256]{1,0:T(8,128)S(1)}, bf16[32,256,256]{1,2,0:T(8,128)(2,1)}) fusion(pred[256,256]{0,1:T(8,128)(4,1)S(1)} %iota_compare_fusion, bf16[256,32,128]{0,2,1:T(8,128)(2,1)} %get-tuple-element.25, bf16[256,32,128]{0,2,1:T(8,128)(2,1)} %get-tuple-element.26, bf16[256,32,128]{0,2,1:T(8,128)(2,1)S(1)} %copy-done.9, ...), kind=kOutput, calls=%fused_computation.6 | convolution fusion | flops 1096802304 | bytes 12681216 | tf_op jit(solution)/shard_map/thf,shf->hts/dot_general | solution.py:70
  107.3 5.8 %fusion.6 = f32[32,256,128]{1,2,0:T(8,128)} fusion(bf16[32,256,256]{1,2,0:T(8,128)(2,1)} %get-tuple-element.20, pred[256,256]{0,1:T(8,128)(4,1)S(1)} %iota_compare_fusion, bf16[256,32,128]{2,1,0:T(8,128)(2,1)S(1)} %bitcast.140), kind=kOutput, calls=%fused_computation.10 | convolution fusion | flops 538968064 | bytes 10551296 | tf_op jit(solution)/shard_map/hts,she->the/dot_general | solution.py:73
  113.1 16.5 %all-gather.2.cloned.1.call-done = bf16[32,256,128]{2,1,0:T(8,128)(2,1)} async-done(((bf16[8,256,128]{2,1,0:T(8,128)(2,1)}), bf16[32,256,128]{2,1,0:T(8,128)(2,1)}) %all-gather.2.cloned.1.call-update) | async-done | bytes 2097168 | tf_op jit(solution)/shard_map/all_gather | solution.py:65
  129.6 5.1 %fusion.13 = bf16[256,32,128]{0,2,1:T(8,128)(2,1)S(1)} fusion(f32[32,256,128]{1,2,0:T(8,128)} %fusion.6, f32[256,32]{0,1:T(8,128)S(1)} %add_bitcast_fusion, pred[256]{0:T(512)(128)(4,1)S(1)} %iota_compare_fusion.1, bf16[32,256,128]{2,1,0:T(8,128)(2,1)} %all-gather.2.cloned.1.call-done, bf16[256,32,128]{0,2,1:T(8,128)(2,1)} %copy-done.8, ...), kind=kOutput, calls=%fused_computation.19 | convolution fusion | flops 551550976 | bytes 12615936 | tf_op jit(solution)/shard_map/thf,hfe->the/dot_general | solution.py:17
  134.7 3.3 %reshape.185 = bf16[4,64,4096]{1,0,2:T(4,128)(2,1)} reshape(bf16[256,32,128]{0,2,1:T(8,128)(2,1)S(1)} %fusion.13) | data formatting | bytes 4194304 | tf_op jit(solution)/shard_map/reshape | solution.py:81
  138.0 6.6 %copy.74 = bf16[4,64,4096]{2,0,1:T(4,128)(2,1)S(1)} copy(bf16[4,64,4096]{1,0,2:T(4,128)(2,1)} %reshape.185) | data formatting | bytes 4194304 | tf_op jit(solution)/shard_map/reshape | solution.py:81
  145.8 2.5 %copy.75 = bf16[4,64,4096]{2,1,0:T(8,128)(2,1)} copy(bf16[4,64,4096]{2,0,1:T(4,128)(2,1)S(1)} %convolution_convert_fusion) | data formatting | bytes 4194304 | tf_op jit(solution)/shard_map/convert_element_type | solution.py:98
  148.3 3.6 %all-to-all-start = ((bf16[4,64,4096]{2,1,0:T(8,128)(2,1)}), bf16[4,64,4096]{2,1,0:T(8,128)(2,1)S(1)}, u32[]{:S(2)}, u32[]{:S(2)}) async-start(bf16[4,64,4096]{2,1,0:T(8,128)(2,1)} %copy.75), calls=%async_computation.1 | async-start | bytes 4194304 | tf_op jit(solution)/shard_map/all_to_all | solution.py:99
  153.8 16.8 %psum.7 = f32[]{:T(128)} all-reduce(f32[]{:T(128)} %multiply_reduce_fusion), channel_id=1, replica_groups=mesh['group'=8,'dp'=4] {'group'}, use_global_device_ids=true, to_apply=%region_20.21 | all-reduce | flops 1 | bytes 8 | tf_op jit(solution)/shard_map/psum | solution.py:106
  172.4 4.5 %all-to-all-done = bf16[4,64,4096]{2,1,0:T(8,128)(2,1)S(1)} async-done(((bf16[4,64,4096]{2,1,0:T(8,128)(2,1)}), bf16[4,64,4096]{2,1,0:T(8,128)(2,1)S(1)}, u32[]{:S(2)}, u32[]{:S(2)}) %all-to-all-start) | async-done | bytes 2097184 | tf_op jit(solution)/shard_map/all_to_all | solution.py:99
  (71 shorter events, 28.7 us)
Async XLA Ops:
  7.2 1.6 copy-start
  7.2 84.8 %reduce-scatter.2.cloned.1.call-start = ((), (), s32[]{:S(2)}) async-start(), calls=%async_computation.2 | async-start | bytes 5242880 | tf_op jit(solution)/shard_map/reduce_scatter | solution.py:61
  17.1 3.6 %copy-start.12 = (bf16[16,8,32,128]{3,2,1,0:T(8,128)(2,1)S(1)}, bf16[16,8,32,128]{3,2,1,0:T(8,128)(2,1)}, u32[]{:S(2)}) copy-start(bf16[16,8,32,128]{3,2,1,0:T(8,128)(2,1)} %copy.92) | copy-start | bytes 3145732
  19.4 1.0 copy-start.4
  19.4 1.3 copy-start.5
  20.8 3.5 %copy-start.13 = (u32[32]{0:T(128)S(1)}, u32[32]{0:T(128)}, u32[]{:S(2)}) copy-start(u32[32]{0:T(128)} %constant.66) | copy-start | bytes 388
  20.8 5.2 %copy-start.14 = (s32[1,2]{1,0:T(1,128)S(1)}, s32[1,2]{1,0:T(1,128)}, u32[]{:S(2)}) copy-start(s32[1,2]{1,0:T(1,128)} %param.18) | copy-start | bytes 28
  23.5 106.1 %all-gather.2.cloned.1.call-start = ((), (), s32[]{:S(2)}) async-start(), calls=%async_computation.3 | async-start | bytes 2621440 | tf_op jit(solution)/shard_map/all_gather | solution.py:65
  35.0 5.7 %copy-start.6 = (bf16[1,256,4096]{2,1,0:T(8,128)(2,1)S(1)}, bf16[1,256,4096]{2,1,0:T(8,128)(2,1)}, u32[]{:S(2)}) copy-start(bf16[1,256,4096]{2,1,0:T(8,128)(2,1)} %param.13) | copy-start | bytes 6291460
  84.9 2.0 %copy-start.8 = (bf16[256,32,128]{0,2,1:T(8,128)(2,1)}, bf16[256,32,128]{0,2,1:T(8,128)(2,1)S(1)}, u32[]{:S(2)}) copy-start(bf16[256,32,128]{0,2,1:T(8,128)(2,1)S(1)} %get-tuple-element.27) | copy-start | bytes 6291460
  84.9 2.0 %copy-start.10 = (bf16[256,32,128]{0,2,1:T(8,128)(2,1)}, bf16[256,32,128]{0,2,1:T(8,128)(2,1)S(1)}, u32[]{:S(2)}) copy-start(bf16[256,32,128]{0,2,1:T(8,128)(2,1)S(1)} %get-tuple-element.28) | copy-start | bytes 6291460
  86.9 2.0 %copy-start.2 = (f32[32,128,256]{2,1,0:T(8,128)}, f32[32,128,256]{2,1,0:T(8,128)S(1)}, u32[]{:S(2)}) copy-start(f32[32,128,256]{2,1,0:T(8,128)S(1)} %fusion.29) | copy-start | bytes 12582916
  94.1 4.6 %copy-start.3 = (f32[256,32,128]{0,2,1:T(8,128)S(1)}, f32[256,32,128]{0,2,1:T(8,128)}, u32[]{:S(2)}) copy-start(f32[256,32,128]{0,2,1:T(8,128)} %get-tuple-element.12) | copy-start | bytes 12582916
  98.8 3.2 %copy-start.9 = (bf16[256,32,128]{0,2,1:T(8,128)(2,1)S(1)}, bf16[256,32,128]{0,2,1:T(8,128)(2,1)}, u32[]{:S(2)}) copy-start(bf16[256,32,128]{0,2,1:T(8,128)(2,1)} %copy-done.8) | copy-start | bytes 6291460
  98.8 3.2 %copy-start.11 = (bf16[256,32,128]{0,2,1:T(8,128)(2,1)S(1)}, bf16[256,32,128]{0,2,1:T(8,128)(2,1)}, u32[]{:S(2)}) copy-start(bf16[256,32,128]{0,2,1:T(8,128)(2,1)} %copy-done.10) | copy-start | bytes 6291460
  102.0 5.3 %copy-start.7 = (bf16[32,8,32,128]{3,2,1,0:T(8,128)(2,1)S(1)}, bf16[32,8,32,128]{3,2,1,0:T(8,128)(2,1)}, u32[]{:S(2)}) copy-start(bf16[32,8,32,128]{3,2,1,0:T(8,128)(2,1)} %copy.95) | copy-start | bytes 6291460
  148.3 28.6 %all-to-all-start = ((bf16[4,64,4096]{2,1,0:T(8,128)(2,1)}), bf16[4,64,4096]{2,1,0:T(8,128)(2,1)S(1)}, u32[]{:S(2)}, u32[]{:S(2)}) async-start(bf16[4,64,4096]{2,1,0:T(8,128)(2,1)} %copy.75), calls=%async_computation.1 | async-start | bytes 4194304 | tf_op jit(solution)/shard_map/all_to_all | solution.py:99
  152.0 28.4 %copy-start.1 = (bf16[32,128,128]{2,1,0:T(8,128)(2,1)S(1)}, bf16[32,128,128]{2,1,0:T(8,128)(2,1)}, u32[]{:S(2)}) copy-start(bf16[32,128,128]{2,1,0:T(8,128)(2,1)} %param.21) | copy-start | bytes 3145732
Sparse Core Ops, SparseCore 0:
  23.7 56.5 reduce-scatter.1
  94.2 35.3 all-gather.1
where the time goes:
time: 188 us; the launch traced here: 187 us
  blocking collectives  51.1 us (27%)
  local copies, waits for them, and re-layouts  31.5 us (17%)
  matrix products  30.7 us (16%)
  other arithmetic  30.3 us (16%)
  waiting for transfers between devices  21.1 us (11%)
  between operations  18.8 us (10%)
  starting transfers between devices  3.69 us (2%)
    unnamed x2, blocking collectives  25.6 us
    psum x1, blocking collectives, body(): spread = lax.psum(jnp.sum(centred * centred), 'group')  16.8 us
    unnamed x41, local copies, waits for them, and re-layouts  16.8 us
    all_gather x1, waiting for transfers between devices, body(): lax.all_gather(kv_share.astype(jnp.bfloat16), 'dp', axis=0, tiled=True)  16.5 us
    sub x3, other arithmetic, features(): jax.nn.softmax(logits, axis=-1)  10.2 us
    reshape x2, local copies, waits for them, and re-layouts, body(): combined.astype(jnp.bfloat16).reshape(-1, BLK, head_count * head_width)  9.89 us
    all_gather x1, blocking collectives, body(): lax.all_gather(total_share.astype(jnp.bfloat16), 'dp', axis=0, tiled=True)  8.64 us
    sub x2, other arithmetic, features(): jax.nn.softmax(-logits, axis=-1)  7.03 us
  transfers between devices with their start and end apart: 3, of which 2 were waited for; matrix products, arithmetic and copies ran while one was open for 27% of the time, Pallas kernels for 0%

commit v1 on v0

v1 whole, which is shorter than its diff:
```python
import functools

import jax
import jax.numpy as jnp
from jax import lax
from jax.experimental import pallas as pl
from jax.experimental.pallas import tpu as pltpu
from jax.sharding import PartitionSpec as P

BLK = 64
MESH = pl.DeviceIdType.MESH
NT = (((1,), (1,)), ((), ()))
NN = (((1,), (0,)), ((), ()))
F32 = jnp.float32
BF16 = jnp.bfloat16


def dot(a, b, dims=NN):
    return lax.dot_general(a, b, dims, preferred_element_type=F32)


def features(rows, weights, ones_blocks):
    logits = dot(rows, weights)
    top = jnp.max(logits, axis=-1, keepdims=True)
    low = jnp.min(logits, axis=-1, keepdims=True)
    both = jnp.concatenate([jnp.exp(logits - top), jnp.exp(low - logits)], axis=1)
    sums = dot(both.astype(BF16), ones_blocks)
    return (both * (1.0 / sums)).astype(BF16)


def kernel(
    n, groups, heads, chunks,
    plen, rlen, slots_sm, rew_sm, q_hbm, k_hbm, v_hbm, pk_hbm, pv_hbm, fq_hbm, fk_hbm,
    out_ref, adv_ref,
    qs, ks, vs, fqs, fks, kbuf, vbuf, state, totals, phq, inum, ostage, orecv,
    tinfo, trew, tsm, gsum,
    load_sem, self_sem, kv_send, kv_recv, st_send, st_recv, o_send, o_recv,
    i_send, i_recv, g_send, g_recv, sm_sem,
):
    me = lax.axis_index("dp")
    grp = lax.axis_index("group")
    rows = qs.shape[0]
    width = fqs.shape[2]
    pieces = rows // BLK
    slot_count = slots_sm.shape[1]
    own = heads // n
    per = own // chunks
    prows = pk_hbm.shape[1]

    def peer(i):
        return lax.rem(me + i, n)

    def source(i):
        return lax.rem(me + (n - i), n)

    loads = [
        pltpu.make_async_copy(src, dst, load_sem.at[i])
        for i, (src, dst) in enumerate(
            [(fq_hbm, fqs), (fk_hbm, fks), (q_hbm.at[0], qs), (k_hbm.at[0], ks), (v_hbm.at[0], vs)]
        )
    ]

    lane = lax.broadcasted_iota(jnp.int32, (8, 128), 1)
    info = jnp.where(lane == slot_count, rlen[0, 0], 0)
    for j in range(slot_count):
        info = jnp.where(lane == j, slots_sm[0, j], info)
    tinfo[me] = info
    trew[me] = jnp.full((8, 128), rew_sm[0, 0], F32)

    barrier = pltpu.get_barrier_semaphore()
    for i in range(1, n):
        pl.semaphore_signal(barrier, inc=1, device_id={"dp": peer(i)}, device_id_type=MESH)
    for i in range(1, groups):
        pl.semaphore_signal(
            barrier, inc=1, device_id={"group": lax.rem(grp + i, groups)}, device_id_type=MESH
        )
    for copy in loads:
        copy.start()
    pl.semaphore_wait(barrier, n + groups - 2)

    def remote(src, dst, send, recv, axis, target):
        return pltpu.make_async_remote_copy(
            src_ref=src, dst_ref=dst, send_sem=send, recv_sem=recv,
            device_id={axis: target}, device_id_type=MESH,
        )

    def kv_cols(owner, c):
        return pl.ds(pl.multiple_of((owner * own + c * per) * width, 128), per * width)

    def kv_copies(c, i):
        result = []
        for a, (hbm, buf) in enumerate([(pk_hbm, kbuf), (pv_hbm, vbuf)]):
            src = hbm.at[0, :, kv_cols(peer(i), c)]
            dst = buf.at[c, me]
            if i == 0:
                result.append(pltpu.make_async_copy(src, dst, self_sem.at[c, a]))
            else:
                result.append(
                    remote(src, dst, kv_send.at[c, a, i], kv_recv.at[c, a, i], "dp", peer(i))
                )
        return result

    def info_copies(i):
        return [
            remote(tinfo.at[me], tinfo.at[me], i_send.at[0, i], i_recv.at[0, i], "dp", peer(i)),
            remote(trew.at[me], trew.at[me], i_send.at[1, i], i_recv.at[1, i], "dp", peer(i)),
        ]

    def group_copy(i):
        return remote(
            gsum.at[grp], gsum.at[grp], g_send.at[i], g_recv.at[i], "group",
            lax.rem(grp + i, groups),
        )

    def state_copies(c, i):
        return [
            remote(
                state.at[me, c], state.at[me, c], st_send.at[c, 0, i], st_recv.at[c, 0, i],
                "dp", peer(i),
            ),
            remote(
                totals.at[me, c], totals.at[me, c], st_send.at[c, 1, i], st_recv.at[c, 1, i],
                "dp", peer(i),
            ),
        ]

    def out_cols(step):
        return pl.ds(pl.multiple_of(source(step) * own * width, 128), own * width)

    def out_copy(step, i):
        cols = out_cols(step)
        return remote(
            ostage.at[i - 1, :, cols], orecv.at[me, :, cols], o_send.at[step, i],
            o_recv.at[step, i], "dp", peer(i),
        )

    for i in range(1, n):
        for copy in info_copies(i):
            copy.start()
    for c in range(chunks):
        for i in [*range(1, n), 0]:
            for copy in kv_copies(c, i):
                copy.start()

    feat = fqs.shape[2]
    left = lax.broadcasted_iota(jnp.int32, (2 * feat, 2 * feat), 0) < feat
    upper = lax.broadcasted_iota(jnp.int32, (2 * feat, 2 * feat), 1) < feat
    ones_blocks = jnp.where(left == upper, 1.0, 0.0).astype(BF16)

    for copy in loads:
        copy.wait()

    def intra_head(h):
        cols = pl.ds(pl.multiple_of(h * width, 128), width)
        qf = features(qs[:, cols], fqs[h], ones_blocks)
        kf = features(ks[:, cols], fks[h], ones_blocks)
        phq[h] = qf
        scores = dot(qf, kf, NT)
        causal = lax.broadcasted_iota(jnp.int32, (rows, rows), 0) >= lax.broadcasted_iota(
            jnp.int32, (rows, rows), 1
        )
        weight = jnp.where(causal, scores, 0.0).astype(BF16)
        value = jnp.concatenate([vs[:, cols], jnp.ones((rows, width), BF16)], axis=1)
        inum[h] = dot(weight, value)

    def intra(first, last):
        def step(t, carry):
            intra_head(first + 2 * t)
            intra_head(first + 2 * t + 1)
            return carry

        lax.fori_loop(0, (last - first) // 2, step, 0)

    def states(c):
        for i in range(n):
            for copy in kv_copies(c, i):
                copy.wait() if i == 0 else copy.wait_recv()
        keep = lax.broadcasted_iota(jnp.int32, (n * prows, 2 * feat), 0) < plen[0]
        line = lax.broadcasted_iota(jnp.int32, totals.shape[2:], 0)

        def step(j, carry):
            cols = pl.ds(pl.multiple_of(j * width, 128), width)
            keys = kbuf[c, :, :, cols].reshape(n * prows, width)
            values = vbuf[c, :, :, cols].reshape(n * prows, width)
            kf = features(keys, fks[me * own + c * per + j], ones_blocks)
            kf = jnp.where(keep, kf.astype(F32), 0.0).astype(BF16)
            state[me, c, pl.ds(pl.multiple_of(j * width, 128), width), :] = dot(
                values.T, kf
            ).astype(BF16)
            total = dot(jnp.ones((totals.shape[2], n * prows), BF16), kf)
            return jnp.where(line == j, total, carry)

        found = lax.fori_loop(0, per, step, jnp.zeros(totals.shape[2:], F32))
        totals[me, c] = found.astype(BF16)
        for i in range(1, n):
            for copy in state_copies(c, i):
                copy.start()

    marks = [heads * 3 // 8 // 2 * 2, heads * 5 // 8 // 2 * 2]
    bounds = [0] + marks[:chunks] + [heads]
    for c in range(chunks):
        intra(bounds[c], bounds[c + 1])
        states(c)

    for i in range(1, n):
        for copy in info_copies(i):
            copy.wait_recv()
    total_reward = trew[0]
    for d in range(1, n):
        total_reward = total_reward + trew[d]
    mean = total_reward / n
    squares = jnp.zeros((8, 128), F32)
    for d in range(n):
        squares = squares + (trew[d] - mean) * (trew[d] - mean)
    gsum[grp] = squares
    table_copy = pltpu.make_async_copy(tinfo, tsm, sm_sem)
    table_copy.start()
    for i in range(1, groups):
        group_copy(i).start()

    intra(bounds[chunks], heads)
    table_copy.wait()

    piece_of = []
    for i in range(n):
        found = jnp.int32(0)
        for j in range(slot_count):
            ident = tsm[peer(i), 0, j] - me * pieces
            found = jnp.where((ident >= 0) & (ident < pieces), ident, found)
        piece_of.append(found)

    live = lax.broadcasted_iota(jnp.int32, (rows, width), 0) < rlen[0, 0]

    def combine_head(owner, c, j):
        h = owner * own + c * per + j
        tot = totals[owner, c].astype(F32)
        line = lax.broadcasted_iota(jnp.int32, tot.shape, 0)
        tot = jnp.sum(jnp.where(line == j, tot, 0.0), axis=0, keepdims=True)
        right = jnp.broadcast_to(tot, (width, tot.shape[1])).astype(BF16)
        part = state[owner, c, pl.ds(pl.multiple_of(j * width, 128), width), :]
        prompt = dot(phq[h], jnp.concatenate([part, right], axis=0), NT)
        both = prompt.astype(BF16).astype(F32) + inum[h]
        result = jnp.where(live, both[:, :width] / both[:, width:], 0.0)
        cols = pl.ds(pl.multiple_of(h * width, 128), width)
        for i in range(n):
            block = result[:BLK]
            for p in range(1, pieces):
                block = jnp.where(piece_of[i] == p, result[p * BLK : (p + 1) * BLK], block)
            if i == 0:
                orecv[me, :, cols] = block.astype(BF16)
            else:
                ostage[i - 1, :, cols] = block.astype(BF16)

    for step in range(n):
        owner = source(step)
        for c in range(chunks):
            if step > 0:
                for copy in state_copies(c, step):
                    copy.wait_recv()

            def body(j, carry, c=c, owner=owner):
                combine_head(owner, c, j)
                return carry

            lax.fori_loop(0, per, body, 0)
        for i in range(1, n):
            out_copy(step, i).start()

    for i in range(1, groups):
        group_copy(i).wait_recv()
    spread = gsum[0]
    for g in range(1, groups):
        spread = spread + gsum[g]
    scale = jnp.sqrt(spread / (groups * n) + 1e-06)
    adv = jnp.zeros((8, 128), F32)
    for j in range(slot_count):
        ident = slots_sm[0, j]
        src = lax.div(ident, pieces)
        start = lax.rem(ident, pieces) * BLK
        reward = jnp.zeros((8, 128), F32)
        size = jnp.int32(0)
        for d in range(n):
            reward = jnp.where(src == d, trew[d], reward)
            size = jnp.where(src == d, tsm[d, 0, slot_count], size)
        value = jnp.where(start + lane - j * BLK < size, (reward - mean) / scale, 0.0)
        adv = jnp.where((lane >= j * BLK) & (lane < (j + 1) * BLK), value, adv)
    adv_ref[...] = adv[:1]

    for step in range(n):
        for i in range(1, n):
            out_copy(step, i).wait_recv()
    for j in range(slot_count):
        src = lax.div(slots_sm[0, j], pieces)
        out_ref[0, j * BLK : (j + 1) * BLK, :] = orecv[src]

    for i in range(1, n):
        for copy in info_copies(i):
            copy.wait_send()
        for c in range(chunks):
            for copy in kv_copies(c, i) + state_copies(c, i):
                copy.wait_send()
        for step in range(n):
            out_copy(step, i).wait_send()
    for i in range(1, groups):
        group_copy(i).wait_send()


def body(
    resp_q, resp_k, resp_v, prompt_k, prompt_v, prompt_len, resp_len, assign, rewards,
    feat_q, feat_k,
):
    n = lax.axis_size("dp")
    groups = lax.axis_size("group")
    heads, width, feat = feat_q.shape
    rows = resp_q.shape[1]
    prows = prompt_k.shape[1]
    model = resp_q.shape[2]
    own = heads // n
    chunks = 2 if own % 2 == 0 else 1
    per = own // chunks
    slot_count = assign.shape[1]
    lines = -(-per // 16) * 16
    smem = pl.BlockSpec(memory_space=pltpu.SMEM)
    hbm = pl.BlockSpec(memory_space=pl.ANY)
    vmem = pl.BlockSpec(memory_space=pltpu.VMEM)
    dma = pltpu.SemaphoreType.DMA
    return pl.pallas_call(
        functools.partial(kernel, n, groups, heads, chunks),
        out_shape=(
            jax.ShapeDtypeStruct((1, slot_count * BLK, model), BF16),
            jax.ShapeDtypeStruct((1, slot_count * BLK), F32),
        ),
        in_specs=[smem] * 4 + [hbm] * 7,
        out_specs=(vmem, vmem),
        scratch_shapes=[
            pltpu.VMEM((rows, model), BF16),
            pltpu.VMEM((rows, model), BF16),
            pltpu.VMEM((rows, model), BF16),
            pltpu.VMEM((heads, width, feat), BF16),
            pltpu.VMEM((heads, width, feat), BF16),
            pltpu.VMEM((chunks, n, prows, per * width), BF16),
            pltpu.VMEM((chunks, n, prows, per * width), BF16),
            pltpu.VMEM((n, chunks, per * width, 2 * feat), BF16),
            pltpu.VMEM((n, chunks, lines, 2 * feat), BF16),
            pltpu.VMEM((heads, rows, 2 * feat), BF16),
            pltpu.VMEM((heads, rows, 2 * width), F32),
            pltpu.VMEM((n - 1, BLK, model), BF16),
            pltpu.VMEM((n, BLK, model), BF16),
            pltpu.VMEM((n, 8, 128), jnp.int32),
            pltpu.VMEM((n, 8, 128), F32),
            pltpu.SMEM((n, 8, 128), jnp.int32),
            pltpu.VMEM((groups, 8, 128), F32),
            dma((5,)),
            dma((chunks, 2)),
            dma((chunks, 2, n)),
            dma((chunks, 2, n)),
            dma((chunks, 2, n)),
            dma((chunks, 2, n)),
            dma((n, n)),
            dma((n, n)),
            dma((2, n)),
            dma((2, n)),
            dma((groups,)),
            dma((groups,)),
            dma,
        ],
        compiler_params=pltpu.CompilerParams(
            collective_id=0, has_side_effects=True, vmem_limit_bytes=62 * 1024 * 1024
        ),
        name="hedgehog",
    )(
        prompt_len, resp_len, assign, rewards, resp_q, resp_k, resp_v, prompt_k, prompt_v,
        feat_q, feat_k,
    )


def solution(mesh):
    return jax.shard_map(
        body,
        mesh=mesh,
        in_specs=(
            P("group", "dp", None),
            P("group", "dp", None),
            P("group", "dp", None),
            P("group", "dp", None),
            P("group", "dp", None),
            P("group"),
            P("group", "dp"),
            P("group", "dp"),
            P("group", "dp"),
            P(),
            P(),
        ),
        out_specs=(P("group", "dp", None), P("group", "dp")),
        check_vma=False,
    )
```

time: 188 us -> 85 us (0.45)
  Pallas kernels: 0 us -> 79.5 us
  blocking collectives: 51.1 us -> 0 us
  matrix products: 30.7 us -> 0 us
  other arithmetic: 30.3 us -> 0 us
  local copies, waits for them, and re-layouts: 31.5 us -> 2.8 us
  waiting for transfers between devices: 21.1 us -> 0 us
  between operations: 18.8 us -> 2.59 us
  starting transfers between devices: 3.69 us -> 0 us
    pallas_call x0 -> x1, Pallas kernels: none -> 79.5 us  [body(): pl.pallas_call(functools.partial(kernel, n, groups, heads, chunks), out_s...]
    dot_general x10 -> x0, matrix products: 28.2 us -> none  [the longest x1 5.81 us: body(): jnp.einsum('hts,she->the', scores.astype(jnp.bfloat16), values, preferred...]
    unnamed x2 -> x0, blocking collectives: 25.6 us -> none
    sub x5 -> x0, other arithmetic: 17.3 us -> none  [the longest x3 10.2 us: features(): jax.nn.softmax(logits, axis=-1)]
    psum x1 -> x0, blocking collectives: 16.8 us -> none  [body(): spread = lax.psum(jnp.sum(centred * centred), 'group')]
    all_gather x1 -> x0, waiting for transfers between devices: 16.5 us -> none  [body(): lax.all_gather(kv_share.astype(jnp.bfloat16), 'dp', axis=0, tiled=True)]
    unnamed x41 -> x4, local copies, waits for them, and re-layouts: 16.8 us -> 2.8 us
    reshape x2 -> x0, local copies, waits for them, and re-layouts: 9.89 us -> none  [body(): combined.astype(jnp.bfloat16).reshape(-1, BLK, head_count * head_width)]
  transfers between devices with their start and end apart: 3 -> 0, of which waited for: 2 -> 0; matrix products, arithmetic and copies ran while one was open for 27% -> 0% of each run, Pallas kernels for 0% -> 0%
where the time goes in v1:
time: 85 us; the launch traced here: 84.8 us
  Pallas kernels  79.5 us (94%)
  local copies, waits for them, and re-layouts  2.8 us (3%)
  between operations  2.59 us (3%)
    pallas_call x1, Pallas kernels, body(): pl.pallas_call(functools.partial(kernel, n, groups, heads, chunks), out_s...  79.5 us
    unnamed x4, local copies, waits for them, and re-layouts  2.8 us

profile of v1, /device:TPU:0, one launch (start us, length us, event | category | flops | bytes accessed | tf_op | source)
XLA Modules:
  0.0 84.8 jit_solution(10700135884231588177)
XLA Ops:
  2.6 79.5 %hedgehog.1 = (bf16[1,128,4096]{2,1,0:T(8,128)(2,1)}, f32[1,128]{1,0:T(1,128)}) custom-call(s32[1]{0:T(128)S(6)} %copy.15.plen, s32[1,1]{1,0:T(1,128)S(6)} %copy.16.rlen, s32[1,2]{1,0:T(1,128)} %slots_sm.1, f32[1,1]{1,0:T(1,128)S(6)} %copy.17.rew_sm, bf16[1,256,4096]{2,1,0:T(8,128)(2,1)} %q_hbm.1, bf16[1,256,4096]{2,1,0:T(8,128)(2,1)} %k_hbm.1, ...), custom_call_target="tpu_custom_call" | custom-call | tf_op jit(solution)/shard_map/hedgehog/pallas_call | solution.py:327
  82.0 0.0 copy-start
  82.0 2.3 %copy.18 = bf16[1,128,4096]{2,1,0:T(8,128)(2,1)} copy(bf16[1,128,4096]{2,1,0:T(8,128)(2,1)} %get-tuple-element.4) | data formatting | bytes 2097152
  84.3 0.0 copy-done
  84.3 0.5 copy.19
Async XLA Ops:
  82.0 2.3 %copy-start = (f32[1,128]{1,0:T(1,128)S(1)}, f32[1,128]{1,0:T(1,128)}, u32[]{:S(2)}) copy-start(f32[1,128]{1,0:T(1,128)} %get-tuple-element.5) | copy-start | bytes 1540

commit v2 on v1

--- a/solution.py
+++ b/solution.py
@@ -29,12 +29,12 @@
 
 
 def kernel(
-    n, groups, heads, chunks,
+    n, across, groups, heads, chunks,
     plen, rlen, slots_sm, rew_sm, q_hbm, k_hbm, v_hbm, pk_hbm, pv_hbm, fq_hbm, fk_hbm,
-    out_ref, adv_ref,
-    qs, ks, vs, fqs, fks, kbuf, vbuf, state, totals, phq, inum, ostage, orecv,
+    orecv, adv_ref,
+    qs, ks, vs, fqs, fks, kbuf, vbuf, state, phq, inum, ostage,
     tinfo, trew, tsm, gsum,
-    load_sem, self_sem, kv_send, kv_recv, st_send, st_recv, o_send, o_recv,
+    load_sem, self_sem, oself_sem, kv_send, kv_recv, st_send, st_recv, o_send, o_recv,
     i_send, i_recv, g_send, g_recv, sm_sem,
 ):
     me = lax.axis_index("dp")
@@ -47,11 +47,15 @@
     per = own // chunks
     prows = pk_hbm.shape[1]
 
+    down = n // across
+    row = me // across
+    col = me % across
+
     def peer(i):
-        return lax.rem(me + i, n)
+        return (row + i // across) % down * across + (col + i % across) % across
 
     def source(i):
-        return lax.rem(me + (n - i), n)
+        return (row + down - i // across) % down * across + (col + across - i % across) % across
 
     loads = [
         pltpu.make_async_copy(src, dst, load_sem.at[i])
@@ -112,27 +116,36 @@
             lax.rem(grp + i, groups),
         )
 
-    def state_copies(c, i):
-        return [
-            remote(
-                state.at[me, c], state.at[me, c], st_send.at[c, 0, i], st_recv.at[c, 0, i],
-                "dp", peer(i),
-            ),
-            remote(
-                totals.at[me, c], totals.at[me, c], st_send.at[c, 1, i], st_recv.at[c, 1, i],
-                "dp", peer(i),
-            ),
-        ]
+    def state_copy(c, i):
+        dr, dc = i // across, i % across
+        if c % 2 == 0:
+            target, holder = (dr * across, dc) if dr else (dc, 0)
+        else:
+            target, holder = (dc, dr * across) if dc else (dr * across, 0)
+        chunk = state.at[source(holder), c]
+        return remote(chunk, chunk, st_send.at[c, i], st_recv.at[c, i], "dp", peer(target))
+
+    straight = [i for i in range(1, n) if i < across or i % across == 0]
+    relayed = [i for i in range(1, n) if i not in straight]
+
+    def feeds(c):
+        return [i for i in straight if (i < across if c % 2 == 0 else i % across == 0)]
+
+    def relay(c):
+        for i in feeds(c):
+            state_copy(c, i).wait_recv()
+        for i in relayed:
+            state_copy(c, i).start()
 
     def out_cols(step):
         return pl.ds(pl.multiple_of(source(step) * own * width, 128), own * width)
 
     def out_copy(step, i):
         cols = out_cols(step)
-        return remote(
-            ostage.at[i - 1, :, cols], orecv.at[me, :, cols], o_send.at[step, i],
-            o_recv.at[step, i], "dp", peer(i),
-        )
+        src, dst = ostage.at[i, :, cols], orecv.at[me, :, cols]
+        if i == 0:
+            return pltpu.make_async_copy(src, dst, oself_sem.at[step])
+        return remote(src, dst, o_send.at[step, i], o_recv.at[step, i], "dp", peer(i))
 
     for i in range(1, n):
         for copy in info_copies(i):
@@ -176,7 +189,8 @@
             for copy in kv_copies(c, i):
                 copy.wait() if i == 0 else copy.wait_recv()
         keep = lax.broadcasted_iota(jnp.int32, (n * prows, 2 * feat), 0) < plen[0]
-        line = lax.broadcasted_iota(jnp.int32, totals.shape[2:], 0)
+        lines = (state.shape[2] - per * width, 2 * feat)
+        line = lax.broadcasted_iota(jnp.int32, lines, 0)
 
         def step(j, carry):
             cols = pl.ds(pl.multiple_of(j * width, 128), width)
@@ -187,20 +201,22 @@
             state[me, c, pl.ds(pl.multiple_of(j * width, 128), width), :] = dot(
                 values.T, kf
             ).astype(BF16)
-            total = dot(jnp.ones((totals.shape[2], n * prows), BF16), kf)
+            total = dot(jnp.ones((lines[0], n * prows), BF16), kf)
             return jnp.where(line == j, total, carry)
 
-        found = lax.fori_loop(0, per, step, jnp.zeros(totals.shape[2:], F32))
-        totals[me, c] = found.astype(BF16)
-        for i in range(1, n):
-            for copy in state_copies(c, i):
-                copy.start()
-
-    marks = [heads * 3 // 8 // 2 * 2, heads * 5 // 8 // 2 * 2]
-    bounds = [0] + marks[:chunks] + [heads]
+        found = lax.fori_loop(0, per, step, jnp.zeros(lines, F32))
+        state[me, c, per * width :, :] = found.astype(BF16)
+        for i in straight:
+            state_copy(c, i).start()
+
+    bounds = [heads * part // 32 * 2 for part in (0, 6, 9, 12)]
     for c in range(chunks):
         intra(bounds[c], bounds[c + 1])
         states(c)
+    relay(0)
+    if chunks > 1:
+        intra(bounds[2], bounds[3])
+        relay(1)
 
     for i in range(1, n):
         for copy in info_copies(i):
@@ -218,7 +234,7 @@
     for i in range(1, groups):
         group_copy(i).start()
 
-    intra(bounds[chunks], heads)
+    intra(bounds[3] if chunks > 1 else bounds[1], heads)
     table_copy.wait()
 
     piece_of = []
@@ -233,7 +249,7 @@
 
     def combine_head(owner, c, j):
         h = owner * own + c * per + j
-        tot = totals[owner, c].astype(F32)
+        tot = state[owner, c, per * width :, :].astype(F32)
         line = lax.broadcasted_iota(jnp.int32, tot.shape, 0)
         tot = jnp.sum(jnp.where(line == j, tot, 0.0), axis=0, keepdims=True)
         right = jnp.broadcast_to(tot, (width, tot.shape[1])).astype(BF16)
@@ -246,24 +262,20 @@
             block = result[:BLK]
             for p in range(1, pieces):
                 block = jnp.where(piece_of[i] == p, result[p * BLK : (p + 1) * BLK], block)
-            if i == 0:
-                orecv[me, :, cols] = block.astype(BF16)
-            else:
-                ostage[i - 1, :, cols] = block.astype(BF16)
+            ostage[i, :, cols] = block.astype(BF16)
 
     for step in range(n):
         owner = source(step)
         for c in range(chunks):
-            if step > 0:
-                for copy in state_copies(c, step):
-                    copy.wait_recv()
+            if step > 0 and step not in feeds(c):
+                state_copy(c, step).wait_recv()
 
             def body(j, carry, c=c, owner=owner):
                 combine_head(owner, c, j)
                 return carry
 
             lax.fori_loop(0, per, body, 0)
-        for i in range(1, n):
+        for i in [*range(1, n), 0]:
             out_copy(step, i).start()
 
     for i in range(1, groups):
@@ -287,22 +299,24 @@
     adv_ref[...] = adv[:1]
 
     for step in range(n):
-        for i in range(1, n):
-            out_copy(step, i).wait_recv()
-    for j in range(slot_count):
-        src = lax.div(slots_sm[0, j], pieces)
-        out_ref[0, j * BLK : (j + 1) * BLK, :] = orecv[src]
+        for i in range(n):
+            out_copy(step, i).wait_recv() if i else out_copy(step, i).wait()
 
     for i in range(1, n):
         for copy in info_copies(i):
             copy.wait_send()
         for c in range(chunks):
-            for copy in kv_copies(c, i) + state_copies(c, i):
+            for copy in kv_copies(c, i) + [state_copy(c, i)]:
                 copy.wait_send()
         for step in range(n):
             out_copy(step, i).wait_send()
     for i in range(1, groups):
         group_copy(i).wait_send()
+
+
+def pick(slots, block_ref, adv_ref, out_ref, adv_out_ref):
+    out_ref[...] = block_ref[...]
+    adv_out_ref[...] = adv_ref[...]
 
 
 def body(
@@ -324,14 +338,15 @@
     hbm = pl.BlockSpec(memory_space=pl.ANY)
     vmem = pl.BlockSpec(memory_space=pltpu.VMEM)
     dma = pltpu.SemaphoreType.DMA
-    return pl.pallas_call(
-        functools.partial(kernel, n, groups, heads, chunks),
+    across = max(b for b in range(1, n + 1) if n % b == 0 and b * b <= n)
+    arrived, adv = pl.pallas_call(
+        functools.partial(kernel, n, across, groups, heads, chunks),
         out_shape=(
-            jax.ShapeDtypeStruct((1, slot_count * BLK, model), BF16),
+            jax.ShapeDtypeStruct((n, BLK, model), BF16),
             jax.ShapeDtypeStruct((1, slot_count * BLK), F32),
         ),
         in_specs=[smem] * 4 + [hbm] * 7,
-        out_specs=(vmem, vmem),
+        out_specs=(hbm, vmem),
         scratch_shapes=[
             pltpu.VMEM((rows, model), BF16),
             pltpu.VMEM((rows, model), BF16),
@@ -340,11 +355,9 @@
             pltpu.VMEM((heads, width, feat), BF16),
             pltpu.VMEM((chunks, n, prows, per * width), BF16),
             pltpu.VMEM((chunks, n, prows, per * width), BF16),
-            pltpu.VMEM((n, chunks, per * width, 2 * feat), BF16),
-            pltpu.VMEM((n, chunks, lines, 2 * feat), BF16),
+            pltpu.VMEM((n, chunks, per * width + lines, 2 * feat), BF16),
             pltpu.VMEM((heads, rows, 2 * feat), BF16),
             pltpu.VMEM((heads, rows, 2 * width), F32),
-            pltpu.VMEM((n - 1, BLK, model), BF16),
             pltpu.VMEM((n, BLK, model), BF16),
             pltpu.VMEM((n, 8, 128), jnp.int32),
             pltpu.VMEM((n, 8, 128), F32),
@@ -352,10 +365,11 @@
             pltpu.VMEM((groups, 8, 128), F32),
             dma((5,)),
             dma((chunks, 2)),
+            dma((n,)),
             dma((chunks, 2, n)),
             dma((chunks, 2, n)),
-            dma((chunks, 2, n)),
-            dma((chunks, 2, n)),
+            dma((chunks, n)),
+            dma((chunks, n)),
             dma((n, n)),
             dma((n, n)),
             dma((2, n)),
@@ -372,6 +386,28 @@
         prompt_len, resp_len, assign, rewards, resp_q, resp_k, resp_v, prompt_k, prompt_v,
         feat_q, feat_k,
     )
+
+    pieces = rows // BLK
+    return pl.pallas_call(
+        pick,
+        out_shape=(
+            jax.ShapeDtypeStruct((1, slot_count * BLK, model), BF16),
+            jax.ShapeDtypeStruct(adv.shape, F32),
+        ),
+        grid_spec=pltpu.PrefetchScalarGridSpec(
+            num_scalar_prefetch=1,
+            grid=(slot_count,),
+            in_specs=[
+                pl.BlockSpec((1, BLK, model), lambda j, slots: (lax.div(slots[0, j], pieces), 0, 0)),
+                pl.BlockSpec(adv.shape, lambda j, slots: (0, 0)),
+            ],
+            out_specs=(
+                pl.BlockSpec((1, BLK, model), lambda j, slots: (0, j, 0)),
+                pl.BlockSpec(adv.shape, lambda j, slots: (0, 0)),
+            ),
+        ),
+        name="pick",
+    )(assign, arrived, adv)
 
 
 def solution(mesh):

time: 85 us -> 82 us (0.965)
  local copies, waits for them, and re-layouts: 2.8 us -> 0 us
    unnamed x4 -> x0, local copies, waits for them, and re-layouts: 2.8 us -> none
    pallas_call x1 -> x2, Pallas kernels: 79.5 us -> 79.2 us  [the longest x1 76.5 us: body(): pl.pallas_call(functools.partial(kernel, n, across, groups, heads, chunks...]
where the time goes in v2:
time: 82 us; the launch traced here: 81.8 us
  Pallas kernels  79.2 us (97%)
  between operations  2.58 us (3%)
    pallas_call x1, Pallas kernels, body(): pl.pallas_call(functools.partial(kernel, n, across, groups, heads, chunks...  76.5 us
    pallas_call x1, Pallas kernels, body(): pl.pallas_call(pick, out_shape=(jax.ShapeDtypeStruct((1, slot_count * BLK...  2.74 us

profile of v2, /device:TPU:0, one launch (start us, length us, event | category | flops | bytes accessed | tf_op | source)
XLA Modules:
  0.0 81.8 jit_solution(13892350713011941099)
XLA Ops:
  2.6 76.5 %hedgehog.1 = (bf16[4,64,4096]{2,1,0:T(8,128)(2,1)}, f32[1,128]{1,0:T(1,128)}) custom-call(s32[1]{0:T(128)S(6)} %copy.13.plen, s32[1,1]{1,0:T(1,128)S(6)} %copy.14.rlen, s32[1,2]{1,0:T(1,128)} %slots.1, f32[1,1]{1,0:T(1,128)S(6)} %copy.15.rew_sm, bf16[1,256,4096]{2,1,0:T(8,128)(2,1)} %q_hbm.1, bf16[1,256,4096]{2,1,0:T(8,128)(2,1)} %k_hbm.1, ...), custom_call_target="tpu_custom_call" | custom-call | tf_op jit(solution)/shard_map/hedgehog/pallas_call | solution.py:342
  79.0 2.7 %pick.1 = (bf16[1,128,4096]{2,1,0:T(8,128)(2,1)}, f32[1,128]{1,0:T(1,128)}) custom-call(s32[1,2]{1,0:T(1,128)} %slots.1, bf16[4,64,4096]{2,1,0:T(8,128)(2,1)} %get-tuple-element.4.block_ref, f32[1,128]{1,0:T(1,128)} %get-tuple-element.5.adv_ref), custom_call_target="tpu_custom_call" | custom-call | tf_op jit(solution)/shard_map/pick/pallas_call | solution.py:391

commit v3 on v2

--- a/solution.py
+++ b/solution.py
@@ -209,7 +209,7 @@
         for i in straight:
             state_copy(c, i).start()
 
-    bounds = [heads * part // 32 * 2 for part in (0, 6, 9, 12)]
+    bounds = [heads * part // 32 * 2 for part in (0, 7, 11, 14)]
     for c in range(chunks):
         intra(bounds[c], bounds[c + 1])
         states(c)

time: 82 us -> 80.3 us (0.979)
  Pallas kernels: 79.2 us -> 77.6 us
    pallas_call x1, Pallas kernels: 76.5 us -> 74.8 us  [body(): pl.pallas_call(functools.partial(kernel, n, across, groups, heads, chunks...]
where the time goes in v3:
time: 80.3 us; the launch traced here: 80.1 us
  Pallas kernels  77.6 us (97%)
  between operations  2.58 us (3%)
    pallas_call x1, Pallas kernels, body(): pl.pallas_call(functools.partial(kernel, n, across, groups, heads, chunks...  74.8 us
    pallas_call x1, Pallas kernels, body(): pl.pallas_call(pick, out_shape=(jax.ShapeDtypeStruct((1, slot_count * BLK...  2.74 us

profile of v3, /device:TPU:0, one launch (start us, length us, event | category | flops | bytes accessed | tf_op | source)
XLA Modules:
  0.0 80.1 jit_solution(16804583480280842176)
XLA Ops:
  2.6 74.8 %hedgehog.1 = (bf16[4,64,4096]{2,1,0:T(8,128)(2,1)}, f32[1,128]{1,0:T(1,128)}) custom-call(s32[1]{0:T(128)S(6)} %copy.13.plen, s32[1,1]{1,0:T(1,128)S(6)} %copy.14.rlen, s32[1,2]{1,0:T(1,128)} %slots.1, f32[1,1]{1,0:T(1,128)S(6)} %copy.15.rew_sm, bf16[1,256,4096]{2,1,0:T(8,128)(2,1)} %q_hbm.1, bf16[1,256,4096]{2,1,0:T(8,128)(2,1)} %k_hbm.1, ...), custom_call_target="tpu_custom_call" | custom-call | tf_op jit(solution)/shard_map/hedgehog/pallas_call | solution.py:342
  77.4 2.7 %pick.1 = (bf16[1,128,4096]{2,1,0:T(8,128)(2,1)}, f32[1,128]{1,0:T(1,128)}) custom-call(s32[1,2]{1,0:T(1,128)} %slots.1, bf16[4,64,4096]{2,1,0:T(8,128)(2,1)} %get-tuple-element.4.block_ref, f32[1,128]{1,0:T(1,128)} %get-tuple-element.5.adv_ref), custom_call_target="tpu_custom_call" | custom-call | tf_op jit(solution)/shard_map/pick/pallas_call | solution.py:391
